TPU v7x, 32 devices: a whole 2x2x4 slice. The times are simulated.
32 devices in a mesh: dp: 4 (over y, x), expert: 8 (over z, core).
Axes of the slice: x: 2, y: 2, z: 4, core: 2. Of those that a mesh axis runs over, the one named last changes fastest.
Arguments:
- tokens: bfloat16 [8192, 1280], P(('dp', 'expert')), may hold values from -6 to 6
- query_weight: bfloat16 [1280, 1280], P('dp'), may hold values from -0.15625 to 0.15625
- key_weight: bfloat16 [1280, 1280], P('dp'), may hold values from -0.15625 to 0.15625
- value_weight: bfloat16 [1280, 1280], P('dp'), may hold values from -0.15625 to 0.15625
- output_weight: bfloat16 [1280, 1280], P('dp'), may hold values from -0.625 to 0.625
- attn_gain: bfloat16 [1280], P('dp'), may hold values from 0.5 to 1.5
- ffn_gain: bfloat16 [1280], P('dp'), may hold values from 0.5 to 1.5
- router_weight: bfloat16 [1280, 16], P('dp'), may hold values from -0.078125 to 0.078125
- shared_gate: bfloat16 [1280, 896], P('dp'), may hold values from -0.15625 to 0.15625
- shared_up: bfloat16 [1280, 896], P('dp'), may hold values from -0.15625 to 0.15625
- shared_down: bfloat16 [896, 1280], P('dp'), may hold values from -0.25 to 0.25
- expert_gate: bfloat16 [16, 1280, 896], P('expert'), may hold values from -0.15625 to 0.15625
- expert_up: bfloat16 [16, 1280, 896], P('expert'), may hold values from -0.15625 to 0.15625
- expert_down: bfloat16 [16, 896, 1280], P('expert'), may hold values from -2 to 2
- expert_ids: int32 [8192, 7], P(('dp', 'expert')), may hold values from 0 to 15, all different within a row; in each aligned block of 256 rows (0 to 255, 256 to 511, ...) at most 128 rows name the same one
- piece_starts: int32 [32], P(('dp', 'expert')), may hold values from 0 to 128
- out_grad: bfloat16 [8192, 1280], P(('dp', 'expert')), may hold values from -6 to 6
Outputs:
- layer_out: bfloat16 [8192, 1280], P(('dp', 'expert'))
- tokens_grad: bfloat16 [8192, 1280], P(('dp', 'expert'))
- query_weight_grad: float32 [1280, 1280], P('dp')
- key_weight_grad: float32 [1280, 1280], P('dp')
- value_weight_grad: float32 [1280, 1280], P('dp')
- output_weight_grad: float32 [1280, 1280], P('dp')
- attn_gain_grad: float32 [1280], P('dp')
- ffn_gain_grad: float32 [1280], P('dp')
- router_weight_grad: float32 [1280, 16], P('dp')
- shared_gate_grad: float32 [1280, 896], P('dp')
- shared_up_grad: float32 [1280, 896], P('dp')
- shared_down_grad: float32 [896, 1280], P('dp')
- expert_gate_grad: float32 [16, 1280, 896], P('expert', 'dp')
- expert_up_grad: float32 [16, 1280, 896], P('expert', 'dp')
- expert_down_grad: float32 [16, 896, 1280], P('expert', 'dp')
- stat_rms: float32 [32, 3], P(('dp', 'expert'))
Inputs may be any that keep to these rules, and one draw needn't show every extreme that they name: `expert_ids`: within each sequence (aligned blocks of 256 rows) no expert is named by more than 128 rows; each row names 7 different experts. The picture piece of sequence s is tokens piece_starts[s] to piece_starts[s] + 127 of it.
All inputs are finite; a program needn't handle non-finite values.
Results may differ from a plain program's by a relative error of at most 0.023.
Values may be sent and summed in bfloat16 or wider, within the bound.
No kernel may reach another device: no remote copies, remote signals or barrier semaphores. Data moves between devices by JAX's collectives and lax.ppermute only.
A program may use at most 320 MiB of HBM per device.

v0:
```python
import jax
import jax.numpy as jnp
from jax import lax
from jax.sharding import PartitionSpec as P

HEAD_DIM = 128
TOP = 7
EXP_DEV = 2
BF = jnp.bfloat16


def product(first_arg, second_arg):
    return jnp.dot(first_arg, second_arg, preferred_element_type=jnp.float32)


def product_high(first_arg, second_arg):
    return jnp.dot(
        first_arg, second_arg, precision=lax.Precision.HIGHEST, preferred_element_type=jnp.float32
    )


def rotary_tables(length, head_size):
    half_dim = head_size // 2
    frequency = 10000.0 ** (-jnp.arange(half_dim, dtype=jnp.float32) * 2.0 / head_size)
    angles = jnp.arange(length, dtype=jnp.float32)[:, None] * frequency[None, :]
    return (jnp.cos(angles), jnp.sin(angles))


def rotate(tensor, cosine, sine_part):
    half_dim = tensor.shape[-1] // 2
    first_half = tensor[..., :half_dim]
    second_half = tensor[..., half_dim:]
    cos_rows = cosine[:, None, :]
    sin_rows = sine_part[:, None, :]
    return jnp.concatenate(
        [
            first_half * cos_rows - second_half * sin_rows,
            first_half * sin_rows + second_half * cos_rows,
        ],
        axis=-1,
    )


def allowed_mask(length, piece_start, piece_len):
    row_index = jnp.arange(length, dtype=jnp.int32)[:, None]
    col_index = jnp.arange(length, dtype=jnp.int32)[None, :]
    row_inside = (row_index >= piece_start) & (row_index < piece_start + piece_len)
    col_inside = (col_index >= piece_start) & (col_index < piece_start + piece_len)
    return (col_index <= row_index) | row_inside & col_inside


def silu_grad(inputs):
    sigmoid_part = jax.nn.sigmoid(inputs)
    return sigmoid_part * (1.0 + inputs * (1.0 - sigmoid_part))


def high_low(values):
    high = values.astype(BF)
    low = (values - high.astype(jnp.float32)).astype(BF)
    return (high, low)


def body(
    tokens,
    query_weight,
    key_weight,
    value_weight,
    output_weight,
    attn_gain,
    ffn_gain,
    router_weight,
    shared_gate,
    shared_up,
    shared_down,
    expert_gate,
    expert_up,
    expert_down,
    expert_ids,
    piece_starts,
    out_grad,
):
    dp = lax.axis_size("dp")
    owners = lax.axis_size("expert")
    me = lax.axis_index("expert")
    experts = EXP_DEV * owners
    length, width = tokens.shape
    rows = query_weight.shape[0]
    hidden = shared_gate.shape[1]
    head_count = width // HEAD_DIM
    score_scale = HEAD_DIM ** (-0.5)
    piece_len = min(256, length // 2)
    capacity = 8 * length // experts
    chosen = (expert_ids[:, :, None] == jnp.arange(experts, dtype=jnp.int32)).any(axis=1)
    chosen_low = jnp.pad(chosen.astype(BF), ((0, 0), (0, 128 - experts)))
    grads_all = lax.all_gather(
        jnp.concatenate([out_grad, chosen_low], axis=1), "expert", axis=0, tiled=True
    ).reshape(owners, length, width + 128)
    small = jnp.concatenate([router_weight, attn_gain[:, None], ffn_gain[:, None]], axis=1)
    small = jnp.pad(small, ((0, 0), (0, 128 - small.shape[1])))
    first_full = lax.all_gather(
        jnp.concatenate([query_weight, key_weight, value_weight, small], axis=1),
        "dp",
        axis=0,
        tiled=True,
    )
    second_full = lax.all_gather(
        jnp.concatenate(
            [output_weight, shared_gate, shared_up, shared_down.reshape(rows, -1)], axis=1
        ),
        "dp",
        axis=0,
        tiled=True,
    )
    query_full = first_full[:, :width]
    key_full = first_full[:, width : 2 * width]
    value_full = first_full[:, 2 * width : 3 * width]
    small_full = first_full[:, 3 * width :]
    router_full = small_full[:, :experts]
    gain_one_f = small_full[:, experts].astype(jnp.float32)
    gain_two_f = small_full[:, experts + 1].astype(jnp.float32)
    output_full = second_full[:, :width]
    shared_gate_full = second_full[:, width : width + hidden]
    shared_up_full = second_full[:, width + hidden : width + 2 * hidden]
    shared_down_full = second_full[:, width + 2 * hidden :].reshape(hidden, width)
    token_f = tokens.astype(jnp.float32)
    norm_one = lax.rsqrt(jnp.mean(token_f * token_f, axis=-1, keepdims=True) + 1e-06)
    attn_in = (token_f * norm_one * gain_one_f).astype(BF)
    cosine, sine_part = rotary_tables(length, HEAD_DIM)
    query_pre = product(attn_in, query_full).reshape(length, head_count, HEAD_DIM)
    key_pre = product(attn_in, key_full).reshape(length, head_count, HEAD_DIM)
    query_rot = rotate(query_pre, cosine, sine_part).astype(BF)
    key_rot = rotate(key_pre, cosine, sine_part).astype(BF)
    values = product(attn_in, value_full).astype(BF).reshape(length, head_count, HEAD_DIM)
    allowed = allowed_mask(length, piece_starts[0], piece_len)
    scores = (
        jnp.einsum("qhd,khd->hqk", query_rot, key_rot, preferred_element_type=jnp.float32)
        * score_scale
    )
    scores = jnp.where(allowed[None], scores, -1e30)
    row_max = jnp.max(scores, axis=-1, keepdims=True)
    exps = jnp.exp(scores - row_max)
    attn_probs = exps / jnp.sum(exps, axis=-1, keepdims=True)
    probs_low = attn_probs.astype(BF)
    context = jnp.einsum("hqk,khd->qhd", probs_low, values, preferred_element_type=jnp.float32)
    context = context.astype(BF).reshape(length, width)
    attn_out = product(context, output_full)
    residual = token_f + attn_out
    norm_two = lax.rsqrt(jnp.mean(residual * residual, axis=-1, keepdims=True) + 1e-06)
    ffn_in = (residual * norm_two * gain_two_f).astype(BF)
    router_probs = jax.nn.softmax(product(ffn_in, router_full), axis=-1)
    gates = jnp.where(chosen, router_probs, 0.0)
    gates_high, gates_low = high_low(gates)
    sent = jnp.concatenate(
        [ffn_in, gates_high, gates_low, jnp.zeros((length, 128 - 2 * experts), BF)], axis=1
    )
    rows_all = lax.all_gather(sent, "expert", axis=0, tiled=True).reshape(
        owners, length, width + 128
    )
    grad_f = out_grad.astype(jnp.float32)
    shared_gate_act = product(ffn_in, shared_gate_full)
    shared_up_act = product(ffn_in, shared_up_full)
    shared_hidden = (jax.nn.silu(shared_gate_act) * shared_up_act).astype(BF)
    shared_out = product(shared_hidden, shared_down_full)
    shared_hidden_grad = product(out_grad, shared_down_full.T)
    shared_down_grad = product(shared_hidden.T, out_grad)
    shared_gate_act_grad = (shared_hidden_grad * shared_up_act * silu_grad(shared_gate_act)).astype(
        BF
    )
    shared_up_act_grad = (shared_hidden_grad * jax.nn.silu(shared_gate_act)).astype(BF)
    shared_gate_grad = product(ffn_in.T, shared_gate_act_grad)
    shared_up_grad = product(ffn_in.T, shared_up_act_grad)
    shared_in_grad = product(shared_gate_act_grad, shared_gate_full.T) + product(
        shared_up_act_grad, shared_up_full.T
    )
    shared_parts = jnp.concatenate(
        [
            shared_gate_grad.astype(BF),
            shared_up_grad.astype(BF),
            shared_down_grad.astype(BF).reshape(dp * rows, -1),
        ],
        axis=1,
    )
    shared_share = lax.psum_scatter(shared_parts, "dp", scatter_dimension=0, tiled=True)
    own = me * EXP_DEV + jnp.arange(EXP_DEV)
    own_hot = (own[:, None] == jnp.arange(experts)[None, :]).astype(jnp.float32)
    mask = jnp.einsum(
        "ste,oe->ost", grads_all[:, :, width : width + experts].astype(jnp.float32), own_hot
    )
    slot = jnp.cumsum(mask, axis=2) - 1.0
    spread = (
        (slot[:, :, None, :] == jnp.arange(capacity, dtype=jnp.float32)[None, None, :, None])
        & (mask[:, :, None, :] > 0)
    ).astype(BF)
    gates_pair = rows_all[:, :, width : width + experts].astype(jnp.float32) + rows_all[
        :, :, width + experts : width + 2 * experts
    ].astype(jnp.float32)
    gates_own = jnp.einsum("ste,oe->ost", gates_pair, own_hot, precision=lax.Precision.HIGHEST)
    slot_gates = jnp.einsum(
        "osct,ost->osc", spread.astype(jnp.float32), gates_own, precision=lax.Precision.HIGHEST
    )
    take = lambda source: jnp.einsum(
        "osct,std->oscd", spread, source, preferred_element_type=jnp.float32
    ).astype(BF)
    expert_in = take(rows_all[:, :, :width]).reshape(EXP_DEV, owners * capacity, width)
    slot_out_grad = take(grads_all[:, :, :width])
    res_grad = (slot_gates[..., None] * slot_out_grad.astype(jnp.float32)).astype(BF)
    res_grad = res_grad.reshape(EXP_DEV, owners * capacity, width)
    mm = lambda spec, a, b: jnp.einsum(spec, a, b, preferred_element_type=jnp.float32)
    routed_gate = mm("erd,edf->erf", expert_in, expert_gate)
    routed_up = mm("erd,edf->erf", expert_in, expert_up)
    routed_hidden = (jax.nn.silu(routed_gate) * routed_up).astype(BF)
    hidden_grad = mm("erd,efd->erf", res_grad, expert_down)
    routed_gate_grad = (hidden_grad * routed_up * silu_grad(routed_gate)).astype(BF)
    routed_up_grad = (hidden_grad * jax.nn.silu(routed_gate)).astype(BF)
    expert_in_grad = (
        (
            mm("erf,edf->erd", routed_gate_grad, expert_gate)
            + mm("erf,edf->erd", routed_up_grad, expert_up)
        )
        .astype(BF)
        .reshape(EXP_DEV, owners, capacity, width)
    )
    routed_res = mm("erf,efd->erd", routed_hidden, expert_down).astype(BF)
    routed_res = routed_res.reshape(EXP_DEV, owners, capacity, width)
    slot_gate_grad = jnp.sum(
        routed_res.astype(jnp.float32) * slot_out_grad.astype(jnp.float32), axis=-1
    )
    token_gate_grad = jnp.einsum(
        "osct,osc,oe->ste",
        spread.astype(jnp.float32),
        slot_gate_grad,
        own_hot,
        precision=lax.Precision.HIGHEST,
    )
    gg_high, gg_low = high_low(token_gate_grad)
    in_grad_part = mm("osct,oscd->std", spread, expert_in_grad).astype(BF)
    back = jnp.concatenate(
        [in_grad_part, gg_high, gg_low, jnp.zeros((owners, length, 128 - 2 * experts), BF)], axis=2
    ).reshape(owners * length, width + 128)
    back = lax.psum_scatter(back, "expert", scatter_dimension=0, tiled=True)
    out_part = mm(
        "osct,oscd->std",
        (spread.astype(jnp.float32) * slot_gates[..., None]).astype(BF),
        routed_res,
    ).astype(BF)
    expert_down_part = mm("erf,erd->efd", routed_hidden, res_grad).astype(BF)
    expert_gate_part = mm("erd,erf->edf", expert_in, routed_gate_grad).astype(BF)
    expert_up_part = mm("erd,erf->edf", expert_in, routed_up_grad).astype(BF)
    expert_parts = jnp.concatenate(
        [
            expert_gate_part.reshape(EXP_DEV, dp, rows, hidden),
            expert_up_part.reshape(EXP_DEV, dp, rows, hidden),
            expert_down_part.reshape(EXP_DEV, dp, rows, hidden),
        ],
        axis=0,
    ).transpose(1, 0, 2, 3)
    expert_share = lax.psum_scatter(expert_parts, "dp", scatter_dimension=0, tiled=True)[0]
    expert_share = expert_share.astype(jnp.float32)
    out_sum = lax.psum_scatter(
        out_part.reshape(owners * length, width), "expert", scatter_dimension=0, tiled=True
    )
    routed_in_grad = back[:, :width].astype(jnp.float32)
    probs_grad = back[:, width : width + experts].astype(jnp.float32) + back[
        :, width + experts : width + 2 * experts
    ].astype(jnp.float32)
    logits_grad = router_probs * (
        probs_grad - jnp.sum(router_probs * probs_grad, axis=-1, keepdims=True)
    )
    router_grad = product_high(ffn_in.astype(jnp.float32).T, logits_grad)
    router_in_grad = product_high(logits_grad, router_full.astype(jnp.float32).T)
    ffn_in_grad = shared_in_grad + routed_in_grad + router_in_grad
    ffn_gain_grad = jnp.sum(ffn_in_grad * residual * norm_two, axis=0)
    upstream_two = ffn_in_grad * gain_two_f
    residual_grad = (
        grad_f
        + norm_two * upstream_two
        - residual * norm_two**3 * jnp.mean(upstream_two * residual, axis=-1, keepdims=True)
    )
    attn_out_grad = residual_grad.astype(BF)
    output_grad = product(context.T, attn_out_grad)
    context_grad = (
        product(attn_out_grad, output_full.T).astype(BF).reshape(length, head_count, HEAD_DIM)
    )
    value_grad = mm("hqk,qhd->khd", probs_low, context_grad).astype(BF).reshape(length, width)
    probs_grad_att = mm("qhd,khd->hqk", context_grad, values)
    row_delta = jnp.sum(attn_probs * probs_grad_att, axis=-1, keepdims=True)
    scores_grad = (attn_probs * (probs_grad_att - row_delta)).astype(BF)
    query_grad = mm("hqk,khd->qhd", scores_grad, key_rot) * score_scale
    key_grad = mm("hqk,qhd->khd", scores_grad, query_rot) * score_scale
    query_pre_grad = rotate(query_grad, cosine, -sine_part).astype(BF).reshape(length, width)
    key_pre_grad = rotate(key_grad, cosine, -sine_part).astype(BF).reshape(length, width)
    query_wgrad = product(attn_in.T, query_pre_grad)
    key_wgrad = product(attn_in.T, key_pre_grad)
    value_wgrad = product(attn_in.T, value_grad)
    attn_in_grad = (
        product(query_pre_grad, query_full.T)
        + product(key_pre_grad, key_full.T)
        + product(value_grad, value_full.T)
    )
    attn_gain_grad = jnp.sum(attn_in_grad * token_f * norm_one, axis=0)
    upstream_one = attn_in_grad * gain_one_f
    tokens_grad = (
        residual_grad
        + norm_one * upstream_one
        - token_f * norm_one**3 * jnp.mean(upstream_one * token_f, axis=-1, keepdims=True)
    )
    small_grads = jnp.concatenate(
        [router_grad, attn_gain_grad[:, None], ffn_gain_grad[:, None]], axis=1
    ).astype(BF)
    small_grads = jnp.pad(small_grads, ((0, 0), (0, 128 - small_grads.shape[1])))
    attn_parts = jnp.concatenate(
        [
            query_wgrad.astype(BF),
            key_wgrad.astype(BF),
            value_wgrad.astype(BF),
            output_grad.astype(BF),
            small_grads,
        ],
        axis=1,
    )
    attn_share = lax.psum_scatter(attn_parts, "dp", scatter_dimension=0, tiled=True)
    shared_share = lax.psum(shared_share, "expert").astype(jnp.float32)
    attn_share = lax.psum(attn_share, "expert").astype(jnp.float32)
    moe_out = shared_out + out_sum.astype(jnp.float32)
    stream_out = residual + moe_out
    stat_rms = jnp.stack(
        [
            jnp.sqrt(jnp.mean(attn_out * attn_out)),
            jnp.sqrt(jnp.mean(moe_out * moe_out)),
            jnp.sqrt(jnp.mean(stream_out * stream_out)),
        ]
    )[None, :]
    return (
        stream_out.astype(BF),
        tokens_grad.astype(BF),
        attn_share[:, :width],
        attn_share[:, width : 2 * width],
        attn_share[:, 2 * width : 3 * width],
        attn_share[:, 3 * width : 4 * width],
        attn_share[:, 4 * width + experts],
        attn_share[:, 4 * width + experts + 1],
        attn_share[:, 4 * width : 4 * width + experts],
        shared_share[:, :hidden],
        shared_share[:, hidden : 2 * hidden],
        shared_share[:, 2 * hidden :].reshape(shared_down.shape),
        expert_share[0:2],
        expert_share[2:4],
        expert_share[4:6].reshape(EXP_DEV, shared_down.shape[0], width),
        stat_rms,
    )


def solution(mesh):
    in_specs = (
        P(("dp", "expert"), None),
        P("dp", None),
        P("dp", None),
        P("dp", None),
        P("dp", None),
        P("dp"),
        P("dp"),
        P("dp", None),
        P("dp", None),
        P("dp", None),
        P("dp", None),
        P("expert", None, None),
        P("expert", None, None),
        P("expert", None, None),
        P(("dp", "expert"), None),
        P(("dp", "expert")),
        P(("dp", "expert"), None),
    )
    out_specs = (
        P(("dp", "expert"), None),
        P(("dp", "expert"), None),
        P("dp", None),
        P("dp", None),
        P("dp", None),
        P("dp", None),
        P("dp"),
        P("dp"),
        P("dp", None),
        P("dp", None),
        P("dp", None),
        P("dp", None),
        P("expert", "dp", None),
        P("expert", "dp", None),
        P("expert", "dp", None),
        P(("dp", "expert"), None),
    )
    return jax.shard_map(body, mesh=mesh, in_specs=in_specs, out_specs=out_specs, check_vma=False)
```

profile of v0, /device:TPU:0, one launch (start us, length us, event | category | flops | bytes accessed | tf_op | source)
XLA Modules:
  0.0 1105.5 jit_solution(541754291438317677)
XLA Ops:
  21.2 96.2 %all-gather.5.cloned.1.call-done = bf16[1280,3968]{1,0:T(8,128)(2,1)} async-done(((bf16[320,3968]{1,0:T(8,128)(2,1)}), bf16[1280,3968]{1,0:T(8,128)(2,1)}) %all-gather.5.cloned.1.call-update) | async-done | bytes 10158096 | tf_op jit(solution)/shard_map/all_gather | solution.py:100
  119.0 3.5 fusion.21
  125.4 4.2 fusion.25
  136.0 3.9 fusion.38
  142.1 3.7 subtract_convert_fusion.3
  151.9 69.7 %all-gather.7.cloned.1.call-done = bf16[1280,3968]{1,0:T(8,128)(2,1)} async-done(((bf16[320,3968]{1,0:T(8,128)(2,1)}), bf16[1280,3968]{1,0:T(8,128)(2,1)}) %all-gather.7.cloned.1.call-update) | async-done | bytes 10158096 | tf_op jit(solution)/shard_map/all_gather | solution.py:106
  221.5 3.9 multiply_reduce_fusion.3
  230.1 54.0 %all-gather.9.cloned.1.call-done = bf16[2048,1408]{1,0:T(8,128)(2,1)} async-done(((bf16[256,1408]{1,0:T(8,128)(2,1)}), bf16[2048,1408]{1,0:T(8,128)(2,1)}) %all-gather.9.cloned.1.call-update) | async-done | bytes 5767184 | tf_op jit(solution)/shard_map/all_gather | solution.py:95
  286.9 58.7 %all-gather.11.cloned.1.call-done = bf16[2048,1408]{0,1:T(8,128)(2,1)} async-done(((bf16[256,1408]{0,1:T(8,128)(2,1)}), bf16[2048,1408]{0,1:T(8,128)(2,1)}) %all-gather.11.cloned.1.call-update) | async-done | bytes 5767184 | tf_op jit(solution)/shard_map/all_gather | solution.py:156
  345.7 5.1 copy.343
  356.1 5.1 fusion.1
  364.0 8.6 copy.341
  372.6 4.6 fusion.12
  377.7 11.8 %fusion.136 = f32[2,1024,896]{2,1,0:T(8,128)} fusion(bf16[2,1024,1280]{2,1,0:T(8,128)(2,1)S(1)} %bitcast.159, bf16[2,1280,896]{2,1,0:T(8,128)(2,1)} %param.28), kind=kOutput, calls=%fused_computation.225 | convolution fusion | flops 4697620480 | bytes 17170432 | tf_op jit(solution)/shard_map/erd,edf->erf/dot_general | solution.py:208
  389.6 7.6 fusion.137
  397.2 14.7 %multiply_convert_fusion = (bf16[2,1024,896]{2,1,0:T(8,128)(2,1)}, bf16[2,1024,896]{2,1,0:T(8,128)(2,1)}, bf16[2,1024,896]{2,1,0:T(8,128)(2,1)}) fusion(f32[2,1024,896]{2,1,0:T(8,128)} %fusion.136, f32[2,1024,896]{2,1,0:T(8,128)} %fusion.137, bf16[2,1024,1280]{2,1,0:T(8,128)(2,1)} %bitcast.163, bf16[2,896,1280]{2,1,0:T(8,128)(2,1)S(1)} %bitcast.194), kind=kOutput, calls=%fused_computation.18 | convolution fusion | flops 4725145600 | bytes 35520512 | tf_op jit(solution)/shard_map/erd,efd->erf/dot_general | solution.py:208
  412.0 7.5 convolution_convert_fusion.5
  425.1 11.4 %fusion.138 = f32[2,1024,1280]{2,1,0:T(8,128)} fusion(bf16[2,1024,896]{2,1,0:T(8,128)(2,1)} %get-tuple-element.115, bf16[2,1280,896]{2,1,0:T(8,128)(2,1)} %param.28), kind=kOutput, calls=%fused_computation.227 | convolution fusion | flops 4697620480 | bytes 18743296 | tf_op jit(solution)/shard_map/erf,edf->erd/dot_general | solution.py:208
  436.5 9.9 add_convert_fusion
  446.4 4.0 bitcast_convert_fusion
  450.5 10.0 concatenate.54
  460.5 8.2 copy.328
  468.7 5.2 bitcast_convert_fusion.1
  473.9 7.9 copy.327
  483.5 3.6 reshape.318
  495.8 3.6 reshape.331
  499.4 3.2 copy.277
  506.9 5.6 pad_maximum_fusion.1
  512.6 10.0 copy.332
  527.3 4.5 reduce-scatter.14.cloned.1.call-done
  537.1 55.2 %reduce-scatter.12.cloned.1.call-done = bf16[256,1280]{0,1:T(8,128)(2,1)} async-done(((bf16[2048,1280]{0,1:T(8,128)(2,1)}), bf16[256,1280]{0,1:T(8,128)(2,1)}) %reduce-scatter.12.cloned.1.call-update) | async-done | bytes 655376 | tf_op jit(solution)/shard_map/reduce_scatter | solution.py:259
  592.3 4.9 multiply_reduce_fusion.2
  598.9 4.5 fusion.41
  614.2 3.2 fusion.19
  617.5 3.4 fusion.35
  638.7 18.6 %copy.330 = bf16[1280,5248]{1,0:T(8,128)(2,1)} copy(bf16[1280,5248]{0,1:T(8,128)(2,1)} %fusion.84) | data formatting | bytes 26869760
  657.3 10.8 convolution_convert_fusion.7
  668.1 9.1 reshape.335
  677.2 10.0 convolution_convert_fusion.9
  687.2 8.4 convolution_convert_fusion.8
  695.7 6.9 copy_bitcast_fusion
  703.0 4.1 copy.333
  707.0 92.5 %reduce-scatter.16.cloned.1.call-done = bf16[320,5248]{1,0:T(8,128)(2,1)} async-done(((bf16[1280,5248]{1,0:T(8,128)(2,1)}), bf16[320,5248]{1,0:T(8,128)(2,1)}) %reduce-scatter.16.cloned.1.call-update) | async-done | bytes 3358736
  799.5 6.1 copy.331
  812.3 120.6 %reduce-scatter.20.cloned.1.call-done = bf16[1,6,320,896]{3,2,1,0:T(8,128)(2,1)} async-done(((bf16[4,6,320,896]{3,2,1,0:T(8,128)(2,1)}), bf16[1,6,320,896]{3,2,1,0:T(8,128)(2,1)}) %reduce-scatter.20.cloned.1.call-update) | async-done | bytes 3440656
  941.7 125.9 %all-reduce.7.cloned.1.call-done = (bf16[320,2688]{0,1:T(8,128)(2,1)}, bf16[320,5248]{0,1:T(8,128)(2,1)}) async-done(((bf16[320,2688]{0,1:T(8,128)(2,1)}, bf16[320,5248]{0,1:T(8,128)(2,1)}), (bf16[320,2688]{0,1:T(8,128)(2,1)}, bf16[320,5248]{0,1:T(8,128)(2,1)})) %all-reduce.7.cloned.1.call-update) | async-done | bytes 5079056 | tf_op jit(solution)/shard_map/psum | solution.py:322
  1067.6 5.0 fusion.130
  1072.6 3.7 convert_element_type.286
  (282 shorter events, 144.2 us)
Async XLA Ops:
  7.2 110.3 %all-gather.5.cloned.1.call-start = ((), (), s32[]{:S(2)}) async-start(), calls=%async_computation.5 | async-start | bytes 12697600 | tf_op jit(solution)/shard_map/all_gather | solution.py:100
  9.4 3.0 copy-start.37
  12.4 209.2 %all-gather.7.cloned.1.call-start = ((), (), s32[]{:S(2)}) async-start(), calls=%async_computation.6 | async-start | bytes 12697600 | tf_op jit(solution)/shard_map/all_gather | solution.py:106
  15.5 268.7 %all-gather.9.cloned.1.call-start = ((), (), s32[]{:S(2)}) async-start(), calls=%async_computation.7 | async-start | bytes 6488064 | tf_op jit(solution)/shard_map/all_gather | solution.py:95
  17.5 328.2 %all-gather.11.cloned.1.call-start = ((), (), s32[]{:S(2)}) async-start(), calls=%async_computation.8 | async-start | bytes 6488064 | tf_op jit(solution)/shard_map/all_gather | solution.py:156
  17.8 208.1 %copy-start.3 = (bf16[256,1280]{0,1:T(8,128)(2,1)}, bf16[256,1280]{0,1:T(8,128)(2,1)S(1)}, u32[]{:S(2)}) copy-start(bf16[256,1280]{0,1:T(8,128)(2,1)S(1)} %copy.227) | copy-start | bytes 1966084
  19.3 103.2 %copy-start.53 = (f32[256]{0:T(256)}, f32[256]{0:T(256)S(1)}, u32[]{:S(2)}) copy-start(f32[256]{0:T(256)S(1)} %get-tuple-element.151) | copy-start | bytes 3076
  21.2 120.9 %copy-start.24 = (f32[256,64]{1,0:T(8,128)}, f32[256,64]{1,0:T(8,128)S(1)}, u32[]{:S(2)}) copy-start(f32[256,64]{1,0:T(8,128)S(1)} %get-tuple-element.156) | copy-start | bytes 196612
  119.0 3.5 copy-start.44
  119.0 107.7 %copy-start.42 = (f32[1280]{0:T(1024)}, f32[1280]{0:T(1024)S(1)}, u32[]{:S(2)}) copy-start(f32[1280]{0:T(1024)S(1)} %get-tuple-element.96) | copy-start | bytes 15364
  229.9 301.9 %reduce-scatter.14.cloned.1.call-start = ((), (), s32[]{:S(2)}) async-start(), calls=%async_computation.10 | async-start | bytes 6488064 | tf_op jit(solution)/shard_map/reduce_scatter | solution.py:240
  350.8 5.3 slice-start.8
  350.9 5.3 slice-start.9
  377.2 12.4 %slice-start.12 = ((s8[4587520]{0:T(1024)(128)(4,1)}), s8[393216]{0:T(1024)(128)(4,1)S(1)}, s32[]{:S(2)}) async-start(s8[4587520]{0:T(1024)(128)(4,1)} %bitcast.195), calls=%async_computation.27 | async-start | bytes 786432
  377.7 11.9 %copy-start.12 = (bf16[2,8,128,1280]{3,2,1,0:T(8,128)(2,1)}, bf16[2,8,128,1280]{3,2,1,0:T(8,128)(2,1)S(1)}, u32[]{:S(2)}) copy-start(bf16[2,8,128,1280]{3,2,1,0:T(8,128)(2,1)S(1)} %copy.246) | copy-start | bytes 15728644
  377.7 11.9 %slice-start.13 = ((s8[4587520]{0:T(1024)(128)(4,1)}), s8[4194304]{0:T(1024)(128)(4,1)S(1)}, s32[]{:S(2)}) async-start(s8[4587520]{0:T(1024)(128)(4,1)} %bitcast.195), calls=%async_computation.28 | async-start | bytes 8388608
  377.7 19.5 %slice-start.10 = ((s8[4587520]{0:T(1024)(128)(4,1)}), s8[4194304]{0:T(1024)(128)(4,1)S(1)}, s32[]{:S(2)}) async-start(s8[4587520]{0:T(1024)(128)(4,1)} %bitcast.193), calls=%async_computation.25 | async-start | bytes 8388608
  389.6 7.7 slice-start.11
  412.0 7.5 slice-start.3
  412.0 7.5 slice-start.4
  425.1 11.4 %copy-start.55 = (bf16[2,1024,896]{2,1,0:T(8,128)(2,1)S(1)}, bf16[2,1024,896]{2,1,0:T(8,128)(2,1)}, u32[]{:S(2)}) copy-start(bf16[2,1024,896]{2,1,0:T(8,128)(2,1)} %get-tuple-element.114) | copy-start | bytes 11010052
  468.7 123.6 %reduce-scatter.12.cloned.1.call-start = ((), (), s32[]{:S(2)}) async-start(), calls=%async_computation.9 | async-start | bytes 5898240 | tf_op jit(solution)/shard_map/reduce_scatter | solution.py:259
  481.9 221.1 %reduce-scatter.18.cloned.1.call-start = ((), (), s32[]{:S(2)}) async-start(), calls=%async_computation.12 | async-start | bytes 8601600
  522.6 276.9 %reduce-scatter.16.cloned.1.call-start = ((), (), s32[]{:S(2)}) async-start(), calls=%async_computation.11 | async-start | bytes 16793600
  535.2 57.0 %copy-start.2 = (f32[256,1280]{0,1:T(8,128)S(1)}, f32[256,1280]{0,1:T(8,128)}, u32[]{:S(2)}) copy-start(f32[256,1280]{0,1:T(8,128)} %copy-done.1) | copy-start | bytes 3932164
  535.3 57.0 %copy-start.43 = (f32[1280]{0:T(1024)S(1)}, f32[1280]{0:T(1024)}, u32[]{:S(2)}) copy-start(f32[1280]{0:T(1024)} %copy-done.42) | copy-start | bytes 15364
  535.3 57.0 %copy-start.49 = (f32[256]{0:T(256)S(1)}, f32[256]{0:T(256)}, u32[]{:S(2)}) copy-start(f32[256]{0:T(256)} %copy-done.48) | copy-start | bytes 3076
  537.1 60.1 %copy-start.11 = (f32[256,1280]{0,1:T(8,128)}, f32[256,1280]{0,1:T(8,128)S(1)}, u32[]{:S(2)}) copy-start(f32[256,1280]{0,1:T(8,128)S(1)} %convolution_add_fusion) | copy-start | bytes 3932164
  537.1 60.1 %copy-start.51 = (f32[256]{0:T(256)S(1)}, f32[256]{0:T(256)}, u32[]{:S(2)}) copy-start(f32[256]{0:T(256)} %get-tuple-element.152) | copy-start | bytes 3076
  592.3 4.9 copy-start.17
  598.9 5.8 copy-start.28
  598.9 5.8 copy-start.47
  614.2 3.3 copy-start.33
  614.2 3.3 copy-start.32
  614.2 7.5 slice-start.5
  617.5 3.5 copy-start.16
  617.5 3.5 copy-start.31
  617.5 4.6 slice-start.6
  617.5 5.1 slice-start.7
  657.3 275.6 %reduce-scatter.20.cloned.1.call-start = ((), (), s32[]{:S(2)}) async-start(), calls=%async_computation.13 | async-start | bytes 17203200
  677.2 10.0 copy-start.56
  677.2 18.4 %slice-start = ((s8[4587520]{0:T(1024)(128)(4,1)}), s8[4194304]{0:T(1024)(128)(4,1)S(1)}, s32[]{:S(2)}) async-start(s8[4587520]{0:T(1024)(128)(4,1)} %bitcast.156), calls=%async_computation.15 | async-start | bytes 8388608
  687.2 8.5 slice-start.1
  702.7 364.9 %all-reduce.7.cloned.1.call-start = ((), (), s32[]{:S(2)}) async-start(), calls=%async_computation.14 | async-start | bytes 12189696 | tf_op jit(solution)/shard_map/psum | solution.py:322
  935.7 3.1 copy-start.5
  1067.6 5.0 copy-start
  1084.0 4.3 copy-start.6
  1090.1 5.4 copy-start.10
  (33 other events, 61.6 us)
Sparse Core Ops, SparseCore 0:
  12.5 104.9 all-gather.4
  119.3 102.1 all-gather.6
  223.7 60.3 all-gather.8
  286.1 59.4 all-gather.10
  468.8 62.9 reduce-scatter.13
  534.0 58.2 reduce-scatter.11
  595.3 73.4 reduce-scatter.17
  672.0 127.5 reduce-scatter.15
  802.6 130.2 reduce-scatter.19
  935.2 132.3 all-reduce.6
where the time goes:
time: 1120 us; the launch traced here: 1110 us
  waiting for transfers between devices  677 us (60%)
  matrix products  195 us (17%)
  local copies, waits for them, and re-layouts  170 us (15%)
  other arithmetic  43.5 us (4%)
  between operations  18.3 us (2%)
    unnamed x13, waiting for transfers between devices  213 us
    psum x1, waiting for transfers between devices, body(): shared_share = lax.psum(shared_share, 'expert').astype(jnp.float32)  126 us
    dot_general x15, matrix products, body(): jnp.einsum(spec, a, b, preferred_element_type=jnp.float32)  106 us
    all_gather x1, waiting for transfers between devices, body(): lax.all_gather(jnp.concatenate([query_weight, key_weight, value_weight, s...  96.2 us
    unnamed x161, local copies, waits for them, and re-layouts  83.6 us
    all_gather x1, waiting for transfers between devices, body(): lax.all_gather(jnp.concatenate([output_weight, shared_gate, shared_up, sh...  69.7 us
    dot_general x22, matrix products, product(): return jnp.dot(first_arg, second_arg, preferred_element_type=jnp.float32)  64 us
    all_gather x1, waiting for transfers between devices, body(): lax.all_gather(sent, 'expert', axis=0, tiled=True)  58.7 us
  transfers between devices with their start and end apart: 10, of which 9 were waited for; matrix products, arithmetic and copies ran while one was open for 22% of the time, Pallas kernels for 0%

commit v1 on v0

--- a/solution.py
+++ b/solution.py
@@ -319,7 +319,7 @@
         axis=1,
     )
     attn_share = lax.psum_scatter(attn_parts, "dp", scatter_dimension=0, tiled=True)
-    shared_share = lax.psum(shared_share, "expert").astype(jnp.float32)
+    shared_share = lax.all_gather(shared_share, "expert").sum(axis=0).astype(jnp.float32)
     attn_share = lax.psum(attn_share, "expert").astype(jnp.float32)
     moe_out = shared_out + out_sum.astype(jnp.float32)
     stream_out = residual + moe_out

time: 1120 us -> 1190 us (1.062)
  waiting for transfers between devices: 677 us -> 759 us
  local copies, waits for them, and re-layouts: 170 us -> 158 us
    all_gather x0 -> x1, waiting for transfers between devices: none -> 119 us  [body(): lax.all_gather(shared_share, 'expert').sum(axis=0).astype(jnp.float32)]
    psum x1, waiting for transfers between devices: 126 us -> 83.7 us  [body(): attn_share = lax.psum(attn_share, 'expert').astype(jnp.float32)]
    unnamed x161 -> x152, local copies, waits for them, and re-layouts: 83.6 us -> 76.4 us
  transfers between devices with their start and end apart: 10 -> 11, of which waited for: 9 -> 10; matrix products, arithmetic and copies ran while one was open for 22% -> 21% of each run, Pallas kernels for 0% -> 0%
where the time goes in v1:
time: 1190 us; the launch traced here: 1180 us
  waiting for transfers between devices  759 us (64%)
  matrix products  195 us (16%)
  local copies, waits for them, and re-layouts  158 us (13%)
  other arithmetic  50.4 us (4%)
  between operations  18 us (2%)
    unnamed x13, waiting for transfers between devices  217 us
    all_gather x1, waiting for transfers between devices, body(): lax.all_gather(shared_share, 'expert').sum(axis=0).astype(jnp.float32)  119 us
    dot_general x15, matrix products, body(): jnp.einsum(spec, a, b, preferred_element_type=jnp.float32)  106 us
    all_gather x1, waiting for transfers between devices, body(): lax.all_gather(jnp.concatenate([query_weight, key_weight, value_weight, s...  96.3 us
    psum x1, waiting for transfers between devices, body(): attn_share = lax.psum(attn_share, 'expert').astype(jnp.float32)  83.7 us
    unnamed x152, local copies, waits for them, and re-layouts  76.4 us
    all_gather x1, waiting for transfers between devices, body(): lax.all_gather(jnp.concatenate([output_weight, shared_gate, shared_up, sh...  69.6 us
    dot_general x22, matrix products, product(): return jnp.dot(first_arg, second_arg, preferred_element_type=jnp.float32)  64 us
  transfers between devices with their start and end apart: 11, of which 10 were waited for; matrix products, arithmetic and copies ran while one was open for 21% of the time, Pallas kernels for 0%

profile of v1, /device:TPU:0, one launch (start us, length us, event | category | flops | bytes accessed | tf_op | source)
XLA Modules:
  0.0 1181.4 jit_solution(5277755415116283899)
XLA Ops:
  21.2 96.3 %all-gather.7.cloned.1.call-done = bf16[1280,3968]{1,0:T(8,128)(2,1)} async-done(((bf16[320,3968]{1,0:T(8,128)(2,1)}), bf16[1280,3968]{1,0:T(8,128)(2,1)}) %all-gather.7.cloned.1.call-update) | async-done | bytes 10158096 | tf_op jit(solution)/shard_map/all_gather | solution.py:100
  119.1 3.5 fusion.21
  125.5 4.2 fusion.25
  136.1 3.9 fusion.38
  142.2 3.7 subtract_convert_fusion.3
  151.9 69.6 %all-gather.9.cloned.1.call-done = bf16[1280,3968]{1,0:T(8,128)(2,1)} async-done(((bf16[320,3968]{1,0:T(8,128)(2,1)}), bf16[1280,3968]{1,0:T(8,128)(2,1)}) %all-gather.9.cloned.1.call-update) | async-done | bytes 10158096 | tf_op jit(solution)/shard_map/all_gather | solution.py:106
  221.5 3.9 multiply_reduce_fusion.3
  230.1 54.0 %all-gather.11.cloned.1.call-done = bf16[2048,1408]{1,0:T(8,128)(2,1)} async-done(((bf16[256,1408]{1,0:T(8,128)(2,1)}), bf16[2048,1408]{1,0:T(8,128)(2,1)}) %all-gather.11.cloned.1.call-update) | async-done | bytes 5767184 | tf_op jit(solution)/shard_map/all_gather | solution.py:95
  286.9 58.7 %all-gather.13.cloned.1.call-done = bf16[2048,1408]{0,1:T(8,128)(2,1)} async-done(((bf16[256,1408]{0,1:T(8,128)(2,1)}), bf16[2048,1408]{0,1:T(8,128)(2,1)}) %all-gather.13.cloned.1.call-update) | async-done | bytes 5767184 | tf_op jit(solution)/shard_map/all_gather | solution.py:156
  345.7 5.1 copy.333
  356.1 5.1 fusion.1
  363.9 8.7 copy.331
  372.6 4.6 fusion.12
  377.7 11.8 fusion.136
  389.5 7.6 fusion.137
  397.2 14.7 %multiply_convert_fusion = (bf16[2,1024,896]{2,1,0:T(8,128)(2,1)}, bf16[2,1024,896]{2,1,0:T(8,128)(2,1)}, bf16[2,1024,896]{2,1,0:T(8,128)(2,1)}) fusion(f32[2,1024,896]{2,1,0:T(8,128)} %fusion.136, f32[2,1024,896]{2,1,0:T(8,128)} %fusion.137, bf16[2,1024,1280]{2,1,0:T(8,128)(2,1)} %bitcast.165, bf16[2,896,1280]{2,1,0:T(8,128)(2,1)S(1)} %bitcast.196), kind=kOutput, calls=%fused_computation.18 | convolution fusion | flops 4725145600 | bytes 35520512 | tf_op jit(solution)/shard_map/erd,efd->erf/dot_general | solution.py:208
  411.9 7.5 convolution_convert_fusion.5
  425.1 11.3 fusion.138
  436.4 9.9 add_convert_fusion
  446.3 4.1 bitcast_convert_fusion
  450.5 10.0 concatenate.54
  460.5 8.2 copy.318
  468.8 5.2 bitcast_convert_fusion.1
  473.9 7.9 copy.317
  483.6 3.6 reshape.318
  495.9 3.6 reshape.331
  499.4 3.2 copy.269
  507.0 5.7 pad_maximum_fusion.1
  512.7 9.8 copy.322
  527.2 4.6 reduce-scatter.14.cloned.1.call-done
  537.1 55.2 %reduce-scatter.12.cloned.1.call-done = bf16[256,1280]{0,1:T(8,128)(2,1)} async-done(((bf16[2048,1280]{0,1:T(8,128)(2,1)}), bf16[256,1280]{0,1:T(8,128)(2,1)}) %reduce-scatter.12.cloned.1.call-update) | async-done | bytes 655376 | tf_op jit(solution)/shard_map/reduce_scatter | solution.py:259
  592.4 4.9 multiply_reduce_fusion.2
  598.9 4.5 fusion.41
  614.3 3.2 fusion.19
  617.6 3.4 fusion.35
  638.7 18.5 %copy.320 = bf16[1280,5248]{1,0:T(8,128)(2,1)} copy(bf16[1280,5248]{0,1:T(8,128)(2,1)} %fusion.84) | data formatting | bytes 26869760
  657.2 10.9 convolution_convert_fusion.7
  668.1 9.1 reshape.335
  677.2 10.0 convolution_convert_fusion.9
  687.2 8.5 convolution_convert_fusion.8
  695.7 6.9 copy_bitcast_fusion
  703.5 96.1 %reduce-scatter.16.cloned.1.call-done = bf16[320,5248]{1,0:T(8,128)(2,1)} async-done(((bf16[1280,5248]{1,0:T(8,128)(2,1)}), bf16[320,5248]{1,0:T(8,128)(2,1)}) %reduce-scatter.16.cloned.1.call-update) | async-done | bytes 3358736
  799.6 6.1 copy.321
  812.4 120.6 %reduce-scatter.20.cloned.1.call-done = bf16[1,6,320,896]{3,2,1,0:T(8,128)(2,1)} async-done(((bf16[4,6,320,896]{3,2,1,0:T(8,128)(2,1)}), bf16[1,6,320,896]{3,2,1,0:T(8,128)(2,1)}) %reduce-scatter.20.cloned.1.call-update) | async-done | bytes 3440656
  941.7 119.1 %all-gather.15.cloned.1.call-done = bf16[2560,2688]{1,0:T(8,128)(2,1)} async-done(((bf16[320,2688]{1,0:T(8,128)(2,1)}), bf16[2560,2688]{1,0:T(8,128)(2,1)}) %all-gather.15.cloned.1.call-update) | async-done | bytes 13762576 | tf_op jit(solution)/shard_map/all_gather | solution.py:322
  1060.9 7.8 reduce_sum.149
  1071.6 83.7 %all-reduce.6.cloned.1.call-done = bf16[320,5248]{0,1:T(8,128)(2,1)} async-done(((bf16[320,5248]{0,1:T(8,128)(2,1)}), bf16[320,5248]{0,1:T(8,128)(2,1)}) %all-reduce.6.cloned.1.call-update) | async-done | bytes 3358736 | tf_op jit(solution)/shard_map/psum | solution.py:323
  1155.3 4.7 fusion.130
  (276 shorter events, 140.1 us)
Async XLA Ops:
  7.2 110.3 %all-gather.7.cloned.1.call-start = ((), (), s32[]{:S(2)}) async-start(), calls=%async_computation.5 | async-start | bytes 12697600 | tf_op jit(solution)/shard_map/all_gather | solution.py:100
  9.4 3.0 copy-start.34
  12.4 209.2 %all-gather.9.cloned.1.call-start = ((), (), s32[]{:S(2)}) async-start(), calls=%async_computation.6 | async-start | bytes 12697600 | tf_op jit(solution)/shard_map/all_gather | solution.py:106
  15.5 268.7 %all-gather.11.cloned.1.call-start = ((), (), s32[]{:S(2)}) async-start(), calls=%async_computation.7 | async-start | bytes 6488064 | tf_op jit(solution)/shard_map/all_gather | solution.py:95
  17.5 328.2 %all-gather.13.cloned.1.call-start = ((), (), s32[]{:S(2)}) async-start(), calls=%async_computation.8 | async-start | bytes 6488064 | tf_op jit(solution)/shard_map/all_gather | solution.py:156
  17.8 208.1 %copy-start.2 = (bf16[256,1280]{0,1:T(8,128)(2,1)}, bf16[256,1280]{0,1:T(8,128)(2,1)S(1)}, u32[]{:S(2)}) copy-start(bf16[256,1280]{0,1:T(8,128)(2,1)S(1)} %copy.219) | copy-start | bytes 1966084
  19.3 103.3 %copy-start.50 = (f32[256]{0:T(256)}, f32[256]{0:T(256)S(1)}, u32[]{:S(2)}) copy-start(f32[256]{0:T(256)S(1)} %get-tuple-element.149) | copy-start | bytes 3076
  21.2 121.0 %copy-start.21 = (f32[256,64]{1,0:T(8,128)}, f32[256,64]{1,0:T(8,128)S(1)}, u32[]{:S(2)}) copy-start(f32[256,64]{1,0:T(8,128)S(1)} %get-tuple-element.154) | copy-start | bytes 196612
  119.0 3.5 copy-start.41
  119.1 107.7 %copy-start.39 = (f32[1280]{0:T(1024)}, f32[1280]{0:T(1024)S(1)}, u32[]{:S(2)}) copy-start(f32[1280]{0:T(1024)S(1)} %get-tuple-element.96) | copy-start | bytes 15364
  229.9 302.0 %reduce-scatter.14.cloned.1.call-start = ((), (), s32[]{:S(2)}) async-start(), calls=%async_computation.10 | async-start | bytes 6488064 | tf_op jit(solution)/shard_map/reduce_scatter | solution.py:240
  350.8 5.3 slice-start.8
  350.9 5.3 slice-start.9
  377.1 12.3 %slice-start.12 = ((s8[4587520]{0:T(1024)(128)(4,1)}), s8[393216]{0:T(1024)(128)(4,1)S(1)}, s32[]{:S(2)}) async-start(s8[4587520]{0:T(1024)(128)(4,1)} %bitcast.197), calls=%async_computation.28 | async-start | bytes 786432
  377.7 11.8 %copy-start.9 = (bf16[2,8,128,1280]{3,2,1,0:T(8,128)(2,1)}, bf16[2,8,128,1280]{3,2,1,0:T(8,128)(2,1)S(1)}, u32[]{:S(2)}) copy-start(bf16[2,8,128,1280]{3,2,1,0:T(8,128)(2,1)S(1)} %copy.238) | copy-start | bytes 15728644
  377.7 11.8 %slice-start.13 = ((s8[4587520]{0:T(1024)(128)(4,1)}), s8[4194304]{0:T(1024)(128)(4,1)S(1)}, s32[]{:S(2)}) async-start(s8[4587520]{0:T(1024)(128)(4,1)} %bitcast.197), calls=%async_computation.29 | async-start | bytes 8388608
  377.7 19.5 %slice-start.10 = ((s8[4587520]{0:T(1024)(128)(4,1)}), s8[4194304]{0:T(1024)(128)(4,1)S(1)}, s32[]{:S(2)}) async-start(s8[4587520]{0:T(1024)(128)(4,1)} %bitcast.195), calls=%async_computation.26 | async-start | bytes 8388608
  389.5 7.7 slice-start.11
  411.9 7.5 slice-start.3
  411.9 7.5 slice-start.4
  425.1 11.3 copy-start.52
  468.7 123.6 %reduce-scatter.12.cloned.1.call-start = ((), (), s32[]{:S(2)}) async-start(), calls=%async_computation.9 | async-start | bytes 5898240 | tf_op jit(solution)/shard_map/reduce_scatter | solution.py:259
  481.9 220.8 %reduce-scatter.18.cloned.1.call-start = ((), (), s32[]{:S(2)}) async-start(), calls=%async_computation.14 | async-start | bytes 8601600 | tf_op jit(solution)/shard_map/reduce_scatter | solution.py:183
  522.5 277.0 %reduce-scatter.16.cloned.1.call-start = ((), (), s32[]{:S(2)}) async-start(), calls=%async_computation.13 | async-start | bytes 16793600
  535.3 57.1 %copy-start.1 = (f32[256,1280]{0,1:T(8,128)S(1)}, f32[256,1280]{0,1:T(8,128)}, u32[]{:S(2)}) copy-start(f32[256,1280]{0,1:T(8,128)} %copy-done) | copy-start | bytes 3932164
  535.3 57.1 %copy-start.40 = (f32[1280]{0:T(1024)S(1)}, f32[1280]{0:T(1024)}, u32[]{:S(2)}) copy-start(f32[1280]{0:T(1024)} %copy-done.39) | copy-start | bytes 15364
  535.3 57.1 %copy-start.46 = (f32[256]{0:T(256)S(1)}, f32[256]{0:T(256)}, u32[]{:S(2)}) copy-start(f32[256]{0:T(256)} %copy-done.45) | copy-start | bytes 3076
  537.1 60.1 %copy-start.8 = (f32[256,1280]{0,1:T(8,128)}, f32[256,1280]{0,1:T(8,128)S(1)}, u32[]{:S(2)}) copy-start(f32[256,1280]{0,1:T(8,128)S(1)} %convolution_add_fusion) | copy-start | bytes 3932164
  537.1 60.1 %copy-start.48 = (f32[256]{0:T(256)S(1)}, f32[256]{0:T(256)}, u32[]{:S(2)}) copy-start(f32[256]{0:T(256)} %get-tuple-element.150) | copy-start | bytes 3076
  592.3 4.9 copy-start.14
  598.9 5.8 copy-start.25
  598.9 5.8 copy-start.44
  614.3 3.3 copy-start.30
  614.3 3.3 copy-start.29
  614.3 7.5 slice-start.5
  617.5 3.5 copy-start.13
  617.5 3.5 copy-start.28
  617.6 4.6 slice-start.6
  617.6 5.1 slice-start.7
  632.2 2.9 copy-start.20
  657.2 275.8 %reduce-scatter.20.cloned.1.call-start = ((), (), s32[]{:S(2)}) async-start(), calls=%async_computation.15 | async-start | bytes 17203200
  677.2 10.0 copy-start.53
  677.2 18.5 %slice-start = ((s8[4587520]{0:T(1024)(128)(4,1)}), s8[4194304]{0:T(1024)(128)(4,1)S(1)}, s32[]{:S(2)}) async-start(s8[4587520]{0:T(1024)(128)(4,1)} %bitcast.157), calls=%async_computation.16 | async-start | bytes 8388608
  687.2 8.5 slice-start.1
  702.6 358.2 %all-gather.15.cloned.1.call-start = ((), (), s32[]{:S(2)}) async-start(), calls=%async_computation.12 | async-start | bytes 15482880 | tf_op jit(solution)/shard_map/all_gather | solution.py:322
  703.2 452.1 %all-reduce.6.cloned.1.call-start = ((), (), s32[]{:S(2)}) async-start(), calls=%async_computation.11 | async-start | bytes 8060928 | tf_op jit(solution)/shard_map/psum | solution.py:323
  807.8 2.9 copy-start.26
  935.8 3.1 copy-start.4
  (31 other events, 55.9 us)
Sparse Core Ops, SparseCore 0:
  12.5 104.9 all-gather.6
  119.3 102.1 all-gather.8
  223.7 60.3 all-gather.10
  286.1 59.4 all-gather.12
  468.8 62.9 reduce-scatter.13
  534.0 58.2 reduce-scatter.11
  595.3 73.4 reduce-scatter.17
  672.0 127.5 reduce-scatter.15
  802.7 130.2 reduce-scatter.19
  934.5 126.3 all-gather.14
  1063.3 91.9 all-reduce.5
